TPU v7x, 32 devices: a whole 2x2x4 slice. The times are simulated.
32 devices in a mesh: dom: 16 (over z, y, x), spin: 2 (over core).
Axes of the slice: x: 2, y: 2, z: 4, core: 2. Of those that a mesh axis runs over, the one named last changes fastest.
Arguments:
- vectors: float32 [2, 8, 262144], P('spin', None, 'dom'), may hold values from -17 to 17
- basis: float32 [2, 16, 262144], P('spin', None, 'dom'), may hold values from -17 to 17
- potential: float32 [2, 262144], P('spin', 'dom'), may hold values from 1 to 3
- hop_table: bfloat16 [8, 128, 128], replicated, may hold values from -0.25 to 0.25
- soc_table: bfloat16 [2, 128, 128], replicated, may hold values from -0.5 to 0.5
- nbr_block: int32 [2048, 16], P('dom'), may hold values from 0 to 2047, as said below
- nbr_type: int32 [2048, 16], P('dom'), may hold values from 0 to 7
- nbr_count: int32 [2048], P('dom'), may hold values from 1 to 16, as said below
- flip_block: int32 [2048], P('dom'), may hold values from 0 to 2047, as said below
Outputs:
- block_one: float32 [2, 8, 262144], P('spin', None, 'dom')
- block_two: float32 [2, 8, 262144], P('spin', None, 'dom')
- coefs_one: float32 [32, 8], replicated
- coefs_two: float32 [40, 8], replicated
Inputs may be any that keep to these rules, and one draw needn't show every extreme that they name: nbr_block[i, l] equals i + d modulo 2048 with -8 <= d <= 8; slots at or beyond nbr_count[i] are ignored; in slot 0, the first block of each group of 128 has d = -8 and the last has d = 8. `nbr_count`: some block has all 16 slots live. flip_block[i] lies in the same domain as i: flip_block[i] // 128 == i // 128.
All inputs are finite; a program needn't handle non-finite values.
Results may differ from a plain program's by a relative error of at most 0.0033.
Values may be sent and summed in bfloat16 or wider, within the bound.
A program may use at most 64 MiB of HBM per device.

v0:
```python
import jax
import jax.numpy as jnp
from jax import lax
from jax.sharding import PartitionSpec as P

RANGE = 8


def extended_2(cells, sides, width):
    for axis, dim in sides:
        count = lax.axis_size(axis)
        head = lax.slice_in_dim(cells, 0, width, axis=dim)
        tail = lax.slice_in_dim(cells, cells.shape[dim] - width, cells.shape[dim], axis=dim)
        cells = jnp.concatenate(
            [
                lax.ppermute(tail, axis, [(i, (i + 1) % count) for i in range(count)]),
                cells,
                lax.ppermute(head, axis, [((i + 1) % count, i) for i in range(count)]),
            ],
            axis=dim,
        )
    return cells


def partner(block, axis, distance):
    count = lax.axis_size(axis)
    route = []
    for low in range(count):
        high = low | 1 << distance
        if high != low and high < count:
            route += [(low, high), (high, low)]
    return lax.ppermute(block, axis, route)


def inner_rows(left_rows, right_rows):
    return lax.dot_general(
        left_rows, right_rows, (((1,), (1,)), ((), ())), precision=lax.Precision.HIGHEST
    )


def times_rows(coef_matrix, span_rows):
    return lax.dot_general(
        coef_matrix, span_rows, (((0,), (0,)), ((), ())), precision=lax.Precision.HIGHEST
    )


def small_product(left_matrix, right_matrix):
    return jnp.dot(left_matrix, right_matrix, precision=lax.Precision.HIGHEST)


def per_device(
    vectors, basis, potential, hop_table, soc_table, nbr_block, nbr_type, nbr_count, flip_block
):
    block_local = nbr_block.shape[0]
    block_width = hop_table.shape[1]
    type_total = hop_table.shape[0]
    slot_total = nbr_block.shape[1]
    vector_count = vectors.shape[1]
    domain_total = lax.axis_size("dom")
    block_total = block_local * domain_total
    norm_count = float(2 * block_local * block_width * domain_total)
    first_block = lax.axis_index("dom") * block_local
    spin_index = lax.axis_index("spin")
    local_index = jnp.arange(block_local, dtype=jnp.int32)
    offset = (nbr_block - (first_block + local_index)[:, None] + RANGE) % block_total - RANGE
    flat_index = (local_index[:, None] + RANGE + offset) * type_total + nbr_type
    live_mask = (jnp.arange(slot_total, dtype=jnp.int32)[None, :] < nbr_count[:, None]).astype(
        jnp.float32
    )
    flip_local = flip_block - first_block
    soc_own = lax.dynamic_index_in_dim(soc_table, spin_index, 0, keepdims=False)
    onsite = potential[0]

    def apply_operator(field):
        rounded = field.reshape(vector_count, block_local, block_width).astype(jnp.bfloat16)
        extended = extended_2(rounded, (("dom", 1),), RANGE)
        products = jnp.einsum(
            "kjc,tbc->kjtb", extended, hop_table, preferred_element_type=jnp.float32
        )
        products = products.reshape(vector_count, -1, block_width)
        gathered = jnp.take(products, flat_index.reshape(-1), axis=1)
        gathered = gathered.reshape(vector_count, block_local, slot_total, block_width)
        hopping = jnp.sum(gathered * live_mask[None, :, :, None], axis=2)
        other_side = partner(rounded, "spin", 0)
        picked = jnp.take(other_side, flip_local, axis=1)
        flip_term = jnp.einsum("kic,bc->kib", picked, soc_own, preferred_element_type=jnp.float32)
        return onsite[None, :] * field + (hopping + flip_term).reshape(vector_count, -1)

    def orthonormal(span, image):
        span_gram, correlation, image_gram = lax.psum(
            (inner_rows(span, span), inner_rows(span, image), inner_rows(image, image)),
            ("dom", "spin"),
        )
        span_gram = span_gram / norm_count
        first_coef = correlation / norm_count
        image_gram = image_gram / norm_count
        total_coef = 2.0 * first_coef - small_product(span_gram, first_coef)
        twice = image - times_rows(total_coef, span)
        gram_matrix = (
            image_gram
            - small_product(total_coef.T, first_coef)
            - small_product(first_coef.T, total_coef)
            + small_product(total_coef.T, small_product(span_gram, total_coef))
        )
        lower_factor = jnp.linalg.cholesky(gram_matrix)
        new_block = lax.linalg.triangular_solve(lower_factor, twice, left_side=True, lower=True)
        coefs = jnp.concatenate([total_coef, lower_factor.T], axis=0)
        return (new_block, coefs)

    current = vectors[0]
    span = jnp.concatenate([basis[0], current], axis=0)
    block_one, coefs_one = orthonormal(span, apply_operator(current))
    span_two = jnp.concatenate([span, block_one], axis=0)
    block_two, coefs_two = orthonormal(span_two, apply_operator(block_one))
    return (block_one[None], block_two[None], coefs_one, coefs_two)


def solution(mesh):
    return jax.shard_map(
        per_device,
        mesh=mesh,
        in_specs=(
            P("spin", None, "dom"),
            P("spin", None, "dom"),
            P("spin", "dom"),
            P(),
            P(),
            P("dom", None),
            P("dom", None),
            P("dom"),
            P("dom"),
        ),
        out_specs=(P("spin", None, "dom"), P("spin", None, "dom"), P(), P()),
        check_vma=False,
    )
```

profile of v0, /device:TPU:0, one launch (start us, length us, event | category | flops | bytes accessed | tf_op | source)
XLA Modules:
  0.0 202.6 jit_solution(12468295660769314962)
XLA Ops:
  0.6 1.2 copy.121
  1.8 0.6 collective-permute-start.2
  2.4 2.5 %collective-permute-start = (bf16[8,8,128]{2,1,0:T(8,128)(2,1)S(1)}, bf16[8,8,128]{2,1,0:T(8,128)(2,1)S(1)}, u32[]{:S(2)}, u32[]{:S(2)}) collective-permute-start(bf16[8,8,128]{2,1,0:T(8,128)(2,1)S(1)} %get-tuple-element.18), channel_id=1, source_target_pairs={{0,2},{2,4},{4,6},{6,8},{8,10},{10,12},{12,14},{14,16},{16,18},{18... | collective-permute-start | bytes 49160 | tf_op jit(solution)/shard_map/ppermute | solution.py:16
  5.0 4.1 %collective-permute-start.1 = (bf16[8,8,128]{2,1,0:T(8,128)(2,1)S(1)}, bf16[8,8,128]{2,1,0:T(8,128)(2,1)S(1)}, u32[]{:S(2)}, u32[]{:S(2)}) collective-permute-start(bf16[8,8,128]{2,1,0:T(8,128)(2,1)S(1)} %get-tuple-element.19), channel_id=1, source_target_pairs={{2,0},{4,2},{6,4},{8,6},{10,8},{12,10},{14,12},{16,14},{18,16},{20... | collective-permute-start | bytes 49160 | tf_op jit(solution)/shard_map/ppermute | solution.py:18
  9.0 0.7 fusion.40
  10.0 0.7 fusion.25
  10.7 1.2 compare_and_fusion.1
  11.9 4.2 %fusion.1 = f32[24,24]{1,0:T(8,128)} fusion(f32[8,16384]{1,0:T(8,128)} %bitcast.113, f32[16,16384]{1,0:T(8,128)} %bitcast.122), kind=kOutput, calls=%fused_computation.27 | convolution fusion | flops 113639424 | bytes 1575168 | tf_op jit(solution)/shard_map/dot_general | solution.py:36
  16.1 0.8 fusion.8
  16.8 1.4 copy.120
  18.3 7.5 %copy.57 = f32[8,1152,128]{2,0,1:T(8,128)} copy(f32[8,1152,128]{2,1,0:T(8,128)S(1)} %bitcast.120) | data formatting | bytes 9437184 | tf_op jit(solution)/shard_map/reshape | solution.py:80
  25.8 18.1 %gather_fusion = f32[2048,8,128]{2,1,0:T(8,128)} fusion(f32[8,1152,128]{2,0,1:T(8,128)} %copy.57, s32[2048]{0:T(1024)S(1)} %fusion.43), kind=kCustom, calls=%fused_computation.clone | custom fusion | bytes 16785408 | tf_op jit(solution)/shard_map/jit(_take)/gather | solution.py:81
  43.9 9.2 %multiply_reduce_fusion.1 = f32[8,128,128]{2,0,1:T(8,128)S(1)} fusion(f32[128,16]{1,0:T(8,128)S(1)} %fusion.25, f32[2048,8,128]{2,1,0:T(8,128)} %gather_fusion, pred[2048]{0:T(1024)(128)(4,1)S(1)} %compare_and_fusion), kind=kLoop, calls=%fused_computation.8 | loop fusion | flops 6160384 | bytes 8923136 | tf_op jit(solution)/shard_map/reduce_sum | solution.py:83
  53.3 0.7 gather_fusion.1
  54.0 0.9 select_bitcast_fusion.1
  54.9 1.1 fusion.5
  56.0 1.3 convolution_bitcast_fusion.1
  57.3 1.6 fusion.2
  59.0 38.1 %all-reduce.1 = (f32[24,24]{1,0:T(8,128)S(1)}, f32[24,8]{0,1:T(8,128)S(1)}, f32[8,8]{0,1:T(8,128)S(1)}) all-reduce(f32[24,24]{1,0:T(8,128)S(1)} %copy-done.5, f32[24,8]{0,1:T(8,128)S(1)} %fusion.2, f32[8,8]{0,1:T(8,128)S(1)} %convolution_bitcast_fusion.1), channel_id=1, replica_groups=mesh['dom'=16,'spin'=2] {'dom','spin'}, use_global_device_ids=true, to_apply=%region_3.6 | all-reduce | flops 832 | bytes 6656 | tf_op jit(solution)/shard_map/psum | solution.py:90
  97.4 1.2 convolution_subtract_fusion.1
  99.0 0.7 cholesky.44
  99.8 0.6 compare_reduce_fusion.1
  100.4 0.6 fusion.58
  101.1 0.6 custom-call.6
  101.7 0.6 fusion.47
  102.5 2.4 %fusion.3 = f32[32,32]{1,0:T(8,128)} fusion(f32[8,16384]{1,0:T(8,128)S(1)} %fusion.47, f32[8,16384]{1,0:T(8,128)S(1)} %bitcast.117, f32[16,16384]{1,0:T(8,128)S(1)} %bitcast.125), kind=kOutput, calls=%fused_computation.29 | convolution fusion | flops 202375168 | bytes 2101248 | tf_op jit(solution)/shard_map/dot_general | solution.py:36
  104.9 2.3 %collective-permute-start.3 = (bf16[8,8,128]{2,1,0:T(8,128)(2,1)S(1)}, bf16[8,8,128]{2,1,0:T(8,128)(2,1)S(1)}, u32[]{:S(2)}, u32[]{:S(2)}) collective-permute-start(bf16[8,8,128]{2,1,0:T(8,128)(2,1)S(1)} %get-tuple-element.16), channel_id=1, source_target_pairs={{0,2},{2,4},{4,6},{6,8},{8,10},{10,12},{12,14},{14,16},{16,18},{18... | collective-permute-start | bytes 49160 | tf_op jit(solution)/shard_map/ppermute | solution.py:16
  107.2 3.3 %collective-permute-start.4 = (bf16[8,8,128]{2,1,0:T(8,128)(2,1)S(1)}, bf16[8,8,128]{2,1,0:T(8,128)(2,1)S(1)}, u32[]{:S(2)}, u32[]{:S(2)}) collective-permute-start(bf16[8,8,128]{2,1,0:T(8,128)(2,1)S(1)} %get-tuple-element.17), channel_id=1, source_target_pairs={{2,0},{4,2},{6,4},{8,6},{10,8},{12,10},{14,12},{16,14},{18,16},{20... | collective-permute-start | bytes 49160 | tf_op jit(solution)/shard_map/ppermute | solution.py:18
  110.5 0.7 pad_maximum_fusion.8
  111.2 1.0 collective-permute-done.3
  112.2 0.8 fusion.13
  113.0 1.4 copy.119
  114.4 7.5 %copy.73 = f32[8,1152,128]{2,0,1:T(8,128)} copy(f32[8,1152,128]{2,1,0:T(8,128)S(1)} %bitcast.121) | data formatting | bytes 9437184 | tf_op jit(solution)/shard_map/reshape | solution.py:80
  122.0 18.1 %gather_fusion.2 = f32[2048,8,128]{2,1,0:T(8,128)} fusion(f32[8,1152,128]{2,0,1:T(8,128)} %copy.73, s32[2048]{0:T(1024)S(1)} %fusion.43), kind=kCustom, calls=%fused_computation.2.clone | custom fusion | bytes 16785408 | tf_op jit(solution)/shard_map/jit(_take)/gather | solution.py:81
  140.1 9.1 %multiply_reduce_fusion = f32[8,128,128]{2,0,1:T(8,128)S(1)} fusion(f32[128,16]{1,0:T(8,128)S(1)} %fusion.25, f32[2048,8,128]{2,1,0:T(8,128)} %gather_fusion.2, pred[2048]{0:T(1024)(128)(4,1)S(1)} %compare_and_fusion), kind=kLoop, calls=%fused_computation.7 | loop fusion | flops 6160384 | bytes 8923136 | tf_op jit(solution)/shard_map/reduce_sum | solution.py:83
  149.2 1.6 gather_fusion.3
  150.9 0.2 select_bitcast_fusion
  151.1 1.0 fusion
  152.1 1.3 fusion.7
  153.4 1.9 fusion.4
  155.3 40.4 %all-reduce = (f32[32,32]{1,0:T(8,128)S(1)}, f32[32,8]{0,1:T(8,128)S(1)}, f32[8,8]{0,1:T(8,128)S(1)}) all-reduce(f32[32,32]{1,0:T(8,128)S(1)} %copy-done.6, f32[32,8]{0,1:T(8,128)S(1)} %fusion.4, f32[8,8]{0,1:T(8,128)S(1)} %fusion.7), channel_id=1, replica_groups=mesh['dom'=16,'spin'=2] {'dom','spin'}, use_global_device_ids=true, to_apply=%region_9.14 | all-reduce | flops 1344 | bytes 10752 | tf_op jit(solution)/shard_map/psum | solution.py:90
  196.0 1.3 convolution_subtract_fusion
  197.8 0.7 cholesky.55
  198.6 0.6 compare_reduce_fusion
  199.2 0.6 fusion.59
  199.9 0.7 pad_maximum_fusion.9
  200.5 0.6 custom-call.7
  201.2 1.4 convolution_bitcast_fusion
  (49 shorter events, 2.2 us)
Async XLA Ops:
  0.6 15.4 %copy-start = (bf16[8,128,128]{2,1,0:T(8,128)(2,1)S(1)}, bf16[8,128,128]{2,1,0:T(8,128)(2,1)}, u32[]{:S(2)}) copy-start(bf16[8,128,128]{2,1,0:T(8,128)(2,1)} %param.19) | copy-start | bytes 786436
  1.8 51.3 %collective-permute-start.2 = (bf16[8,128,128]{2,1,0:T(8,128)(2,1)S(1)}, bf16[8,128,128]{2,1,0:T(8,128)(2,1)S(1)}, u32[]{:S(2)}, u32[]{:S(2)}) collective-permute-start(bf16[8,128,128]{2,1,0:T(8,128)(2,1)S(1)} %bitcast.137), channel_id=1, source_target_pairs={{0,1},{1,0},{2,3},{3,2},{4,5},{5,4},{6,7},{7,6},{8,9},{9,8},{10,11... | collective-permute-start | bytes 786440 | tf_op jit(solution)/shard_map/ppermute | solution.py:32
  2.4 13.6 %collective-permute-start = (bf16[8,8,128]{2,1,0:T(8,128)(2,1)S(1)}, bf16[8,8,128]{2,1,0:T(8,128)(2,1)S(1)}, u32[]{:S(2)}, u32[]{:S(2)}) collective-permute-start(bf16[8,8,128]{2,1,0:T(8,128)(2,1)S(1)} %get-tuple-element.18), channel_id=1, source_target_pairs={{0,2},{2,4},{4,6},{6,8},{8,10},{10,12},{12,14},{14,16},{16,18},{18... | collective-permute-start | bytes 49160 | tf_op jit(solution)/shard_map/ppermute | solution.py:16
  5.0 11.1 %collective-permute-start.1 = (bf16[8,8,128]{2,1,0:T(8,128)(2,1)S(1)}, bf16[8,8,128]{2,1,0:T(8,128)(2,1)S(1)}, u32[]{:S(2)}, u32[]{:S(2)}) collective-permute-start(bf16[8,8,128]{2,1,0:T(8,128)(2,1)S(1)} %get-tuple-element.19), channel_id=1, source_target_pairs={{2,0},{4,2},{6,4},{8,6},{10,8},{12,10},{14,12},{16,14},{18,16},{20... | collective-permute-start | bytes 49160 | tf_op jit(solution)/shard_map/ppermute | solution.py:18
  43.9 11.0 %copy-start.1 = (f32[1,8,16384]{2,1,0:T(8,128)S(1)}, f32[1,8,16384]{2,1,0:T(8,128)}, u32[]{:S(2)}) copy-start(f32[1,8,16384]{2,1,0:T(8,128)} %param.16) | copy-start | bytes 1572868
  43.9 11.0 %copy-start.4 = (f32[1,16384]{1,0:T(1,128)S(1)}, f32[1,16384]{1,0:T(1,128)}, u32[]{:S(2)}) copy-start(f32[1,16384]{1,0:T(1,128)} %param.18) | copy-start | bytes 196612
  53.3 4.0 %copy-start.2 = (f32[1,16,16384]{2,1,0:T(8,128)S(1)}, f32[1,16,16384]{2,1,0:T(8,128)}, u32[]{:S(2)}) copy-start(f32[1,16,16384]{2,1,0:T(8,128)} %param.17) | copy-start | bytes 3145732
  54.9 4.0 %copy-start.5 = (f32[24,24]{1,0:T(8,128)S(1)}, f32[24,24]{1,0:T(8,128)}, u32[]{:S(2)}) copy-start(f32[24,24]{1,0:T(8,128)} %fusion.1) | copy-start | bytes 6916
  102.3 93.7 %copy-start.3 = (f32[8,16384]{1,0:T(8,128)}, f32[8,16384]{1,0:T(8,128)S(1)}, u32[]{:S(2)}) copy-start(f32[8,16384]{1,0:T(8,128)S(1)} %fusion.47) | copy-start | bytes 1572868
  102.4 46.8 %collective-permute-start.5 = (bf16[8,128,128]{2,0,1:T(8,128)(2,1)S(1)}, bf16[8,128,128]{2,0,1:T(8,128)(2,1)}, u32[]{:S(2)}, u32[]{:S(2)}) collective-permute-start(bf16[8,128,128]{2,0,1:T(8,128)(2,1)S(1)} %convert_bitcast_fusion), channel_id=1, source_target_pairs={{0,1},{1,0},{2,3},{3,2},{4,5},{5,4},{6,7},{7,6},{8,9},{9,8},{10,11... | collective-permute-start | bytes 786440 | tf_op jit(solution)/shard_map/ppermute | solution.py:32
  104.9 7.3 %collective-permute-start.3 = (bf16[8,8,128]{2,1,0:T(8,128)(2,1)S(1)}, bf16[8,8,128]{2,1,0:T(8,128)(2,1)S(1)}, u32[]{:S(2)}, u32[]{:S(2)}) collective-permute-start(bf16[8,8,128]{2,1,0:T(8,128)(2,1)S(1)} %get-tuple-element.16), channel_id=1, source_target_pairs={{0,2},{2,4},{4,6},{6,8},{8,10},{10,12},{12,14},{14,16},{16,18},{18... | collective-permute-start | bytes 49160 | tf_op jit(solution)/shard_map/ppermute | solution.py:16
  107.2 5.1 %collective-permute-start.4 = (bf16[8,8,128]{2,1,0:T(8,128)(2,1)S(1)}, bf16[8,8,128]{2,1,0:T(8,128)(2,1)S(1)}, u32[]{:S(2)}, u32[]{:S(2)}) collective-permute-start(bf16[8,8,128]{2,1,0:T(8,128)(2,1)S(1)} %get-tuple-element.17), channel_id=1, source_target_pairs={{2,0},{4,2},{6,4},{8,6},{10,8},{12,10},{14,12},{16,14},{18,16},{20... | collective-permute-start | bytes 49160 | tf_op jit(solution)/shard_map/ppermute | solution.py:18
  140.1 10.8 %copy-start.7 = (pred[128]{0:T(512)(128)(4,1)S(1)}, pred[128]{0:T(512)(128)(4,1)}, u32[]{:S(2)}) copy-start(pred[128]{0:T(512)(128)(4,1)} %get-tuple-element.14) | copy-start | bytes 388
  152.1 3.2 %copy-start.6 = (f32[32,32]{1,0:T(8,128)S(1)}, f32[32,32]{1,0:T(8,128)}, u32[]{:S(2)}) copy-start(f32[32,32]{1,0:T(8,128)} %fusion.3) | copy-start | bytes 12292
where the time goes:
time: 203 us
  blocking collectives  78.6 us (39%)
  local copies, waits for them, and re-layouts  58.3 us (29%)
  other arithmetic  28.8 us (14%)
  matrix products  22.2 us (11%)
  starting transfers between devices  12.9 us (6%)
    psum x2, blocking collectives, orthonormal(): lax.psum((inner_rows(span, span), inner_rows(span, image), inner_rows(ima...  78.6 us
    gather x2, local copies, waits for them, and re-layouts, apply_operator(): gathered = jnp.take(products, flat_index.reshape(-1), axis=1)  36.3 us
    reduce_sum x2, other arithmetic, apply_operator(): hopping = jnp.sum(gathered * live_mask[None, :, :, None], axis=2)  18.3 us
    reshape x2, local copies, waits for them, and re-layouts, apply_operator(): products = products.reshape(vector_count, -1, block_width)  15.1 us
    dot_general x6, matrix products, inner_rows(): lax.dot_general(left_rows, right_rows, (((1,), (1,)), ((), ())), precisio...  12.6 us
    ppermute x2, starting transfers between devices, extended_2(): lax.ppermute(head, axis, [((i + 1) % count, i) for i in range(count)])  7.41 us
    ppermute x2, starting transfers between devices, extended_2(): lax.ppermute(tail, axis, [(i, (i + 1) % count) for i in range(count)])  4.82 us
  transfers between devices with their start and end apart: 6, of which 1 were waited for; matrix products, arithmetic and copies ran while one was open for 42% of the time, Pallas kernels for 0%

commit v1 on v0

--- a/solution.py
+++ b/solution.py
@@ -2,6 +2,7 @@
 import jax.numpy as jnp
 from jax import lax
 from jax.sharding import PartitionSpec as P
+from jax.lax import psum
 
 RANGE = 8
 
@@ -87,9 +88,11 @@
         return onsite[None, :] * field + (hopping + flip_term).reshape(vector_count, -1)
 
     def orthonormal(span, image):
-        span_gram, correlation, image_gram = lax.psum(
-            (inner_rows(span, span), inner_rows(span, image), inner_rows(image, image)),
-            ("dom", "spin"),
+        span_gram, correlation, image_gram = psum(
+            psum(
+                (inner_rows(span, span), inner_rows(span, image), inner_rows(image, image)), "spin"
+            ),
+            "dom",
         )
         span_gram = span_gram / norm_count
         first_coef = correlation / norm_count

time: 203 us -> 282 us (1.39)
  blocking collectives: 78.6 us -> 158 us
    psum x2 -> x4, blocking collectives: 78.6 us -> 158 us  [the longest x2 151 us: orthonormal(): psum(psum((inner_rows(span, span), inner_rows(span, image), inner_rows(im...]
  transfers between devices with their start and end apart: 6 -> 6, of which waited for: 1 -> 1; matrix products, arithmetic and copies ran while one was open for 42% -> 30% of each run, Pallas kernels for 0% -> 0%
where the time goes in v1:
time: 282 us
  blocking collectives  158 us (56%)
  local copies, waits for them, and re-layouts  58.3 us (21%)
  other arithmetic  28.8 us (10%)
  matrix products  22.2 us (8%)
  starting transfers between devices  12.9 us (5%)
    psum x2, blocking collectives, orthonormal(): psum(psum((inner_rows(span, span), inner_rows(span, image), inner_rows(im...  151 us
    gather x2, local copies, waits for them, and re-layouts, apply_operator(): gathered = jnp.take(products, flat_index.reshape(-1), axis=1)  36.3 us
    reduce_sum x2, other arithmetic, apply_operator(): hopping = jnp.sum(gathered * live_mask[None, :, :, None], axis=2)  18.3 us
    reshape x2, local copies, waits for them, and re-layouts, apply_operator(): products = products.reshape(vector_count, -1, block_width)  15.1 us
    dot_general x6, matrix products, inner_rows(): lax.dot_general(left_rows, right_rows, (((1,), (1,)), ((), ())), precisio...  12.6 us
    ppermute x2, starting transfers between devices, extended_2(): lax.ppermute(head, axis, [((i + 1) % count, i) for i in range(count)])  9.67 us
    psum x2, blocking collectives, orthonormal(): psum((inner_rows(span, span), inner_rows(span, image), inner_rows(image,...  6.84 us
  transfers between devices with their start and end apart: 6, of which 1 were waited for; matrix products, arithmetic and copies ran while one was open for 30% of the time, Pallas kernels for 0%

profile of v1, /device:TPU:0, one launch (start us, length us, event | category | flops | bytes accessed | tf_op | source)
XLA Modules:
  0.0 281.6 jit_solution(2419140348103972456)
XLA Ops:
  0.6 1.2 copy.121
  1.8 0.6 collective-permute-start.2
  2.4 2.5 collective-permute-start
  5.0 4.1 %collective-permute-start.1 = (bf16[8,8,128]{2,1,0:T(8,128)(2,1)S(1)}, bf16[8,8,128]{2,1,0:T(8,128)(2,1)S(1)}, u32[]{:S(2)}, u32[]{:S(2)}) collective-permute-start(bf16[8,8,128]{2,1,0:T(8,128)(2,1)S(1)} %get-tuple-element.25), channel_id=1, source_target_pairs={{2,0},{4,2},{6,4},{8,6},{10,8},{12,10},{14,12},{16,14},{18,16},{20... | collective-permute-start | bytes 49160 | tf_op jit(solution)/shard_map/ppermute | solution.py:19
  9.0 0.7 fusion.40
  10.0 0.7 fusion.25
  10.7 1.2 compare_and_fusion.1
  11.9 4.2 %fusion.1 = f32[24,24]{1,0:T(8,128)} fusion(f32[8,16384]{1,0:T(8,128)} %bitcast.113, f32[16,16384]{1,0:T(8,128)} %bitcast.122), kind=kOutput, calls=%fused_computation.27 | convolution fusion | flops 113639424 | bytes 1575168 | tf_op jit(solution)/shard_map/dot_general | solution.py:37
  16.1 0.8 fusion.8
  16.8 1.4 copy.120
  18.3 7.5 %copy.57 = f32[8,1152,128]{2,0,1:T(8,128)} copy(f32[8,1152,128]{2,1,0:T(8,128)S(1)} %bitcast.120) | data formatting | bytes 9437184 | tf_op jit(solution)/shard_map/reshape | solution.py:81
  25.8 18.1 %gather_fusion = f32[2048,8,128]{2,1,0:T(8,128)} fusion(f32[8,1152,128]{2,0,1:T(8,128)} %copy.57, s32[2048]{0:T(1024)S(1)} %fusion.43), kind=kCustom, calls=%fused_computation.clone | custom fusion | bytes 16785408 | tf_op jit(solution)/shard_map/jit(_take)/gather | solution.py:82
  43.9 9.2 %multiply_reduce_fusion.1 = f32[8,128,128]{2,0,1:T(8,128)S(1)} fusion(f32[128,16]{1,0:T(8,128)S(1)} %fusion.25, f32[2048,8,128]{2,1,0:T(8,128)} %gather_fusion, pred[2048]{0:T(1024)(128)(4,1)S(1)} %compare_and_fusion), kind=kLoop, calls=%fused_computation.8 | loop fusion | flops 6160384 | bytes 8923136 | tf_op jit(solution)/shard_map/reduce_sum | solution.py:84
  53.3 0.7 gather_fusion.1
  54.0 0.9 select_bitcast_fusion.1
  54.9 1.1 fusion.5
  56.0 1.3 convolution_bitcast_fusion.1
  57.3 1.6 fusion.2
  59.0 3.4 %all-reduce.3 = (f32[24,24]{1,0:T(8,128)S(1)}, f32[24,8]{0,1:T(8,128)S(1)}, f32[8,8]{0,1:T(8,128)S(1)}) all-reduce(f32[24,24]{1,0:T(8,128)S(1)} %copy-done.5, f32[24,8]{0,1:T(8,128)S(1)} %fusion.2, f32[8,8]{0,1:T(8,128)S(1)} %convolution_bitcast_fusion.1), channel_id=1, replica_groups=mesh['dom'=16,'spin'=2] {'spin'}, use_global_device_ids=true, to_apply=%region_5.8 | all-reduce | flops 832 | bytes 6656 | tf_op jit(solution)/shard_map/psum | solution.py:92
  62.4 73.5 %all-reduce.1 = (f32[24,24]{1,0:T(8,128)S(1)}, f32[24,8]{0,1:T(8,128)S(1)}, f32[8,8]{0,1:T(8,128)S(1)}) all-reduce(f32[24,24]{1,0:T(8,128)S(1)} %get-tuple-element.17, f32[24,8]{0,1:T(8,128)S(1)} %get-tuple-element.18, f32[8,8]{0,1:T(8,128)S(1)} %get-tuple-element.19), channel_id=1, replica_groups=mesh['dom'=16,'spin'=2] {'dom'}, use_global_device_ids=true, to_apply=%region_6.9 | all-reduce | flops 832 | bytes 6656 | tf_op jit(solution)/shard_map/psum | solution.py:91
  136.2 1.2 convolution_subtract_fusion.1
  137.8 0.7 cholesky.44
  138.6 0.6 compare_reduce_fusion.1
  139.2 0.6 fusion.58
  139.9 0.6 custom-call.6
  140.5 0.6 fusion.47
  141.3 2.4 fusion.3
  143.7 5.6 %collective-permute-start.4 = (bf16[8,8,128]{2,1,0:T(8,128)(2,1)S(1)}, bf16[8,8,128]{2,1,0:T(8,128)(2,1)S(1)}, u32[]{:S(2)}, u32[]{:S(2)}) collective-permute-start(bf16[8,8,128]{2,1,0:T(8,128)(2,1)S(1)} %get-tuple-element.23), channel_id=1, source_target_pairs={{2,0},{4,2},{6,4},{8,6},{10,8},{12,10},{14,12},{16,14},{18,16},{20... | collective-permute-start | bytes 49160 | tf_op jit(solution)/shard_map/ppermute | solution.py:19
  149.3 0.7 pad_maximum_fusion.8
  150.0 1.0 collective-permute-done.3
  151.0 0.8 fusion.13
  151.8 1.4 copy.119
  153.2 7.5 %copy.73 = f32[8,1152,128]{2,0,1:T(8,128)} copy(f32[8,1152,128]{2,1,0:T(8,128)S(1)} %bitcast.121) | data formatting | bytes 9437184 | tf_op jit(solution)/shard_map/reshape | solution.py:81
  160.8 18.1 %gather_fusion.2 = f32[2048,8,128]{2,1,0:T(8,128)} fusion(f32[8,1152,128]{2,0,1:T(8,128)} %copy.73, s32[2048]{0:T(1024)S(1)} %fusion.43), kind=kCustom, calls=%fused_computation.2.clone | custom fusion | bytes 16785408 | tf_op jit(solution)/shard_map/jit(_take)/gather | solution.py:82
  178.9 9.1 %multiply_reduce_fusion = f32[8,128,128]{2,0,1:T(8,128)S(1)} fusion(f32[128,16]{1,0:T(8,128)S(1)} %fusion.25, f32[2048,8,128]{2,1,0:T(8,128)} %gather_fusion.2, pred[2048]{0:T(1024)(128)(4,1)S(1)} %compare_and_fusion), kind=kLoop, calls=%fused_computation.7 | loop fusion | flops 6160384 | bytes 8923136 | tf_op jit(solution)/shard_map/reduce_sum | solution.py:84
  188.1 1.6 gather_fusion.3
  189.9 1.0 fusion
  190.9 1.3 fusion.7
  192.2 1.9 fusion.4
  194.1 3.4 %all-reduce.2 = (f32[32,32]{1,0:T(8,128)S(1)}, f32[32,8]{0,1:T(8,128)S(1)}, f32[8,8]{0,1:T(8,128)S(1)}) all-reduce(f32[32,32]{1,0:T(8,128)S(1)} %copy-done.6, f32[32,8]{0,1:T(8,128)S(1)} %fusion.4, f32[8,8]{0,1:T(8,128)S(1)} %fusion.7), channel_id=1, replica_groups=mesh['dom'=16,'spin'=2] {'spin'}, use_global_device_ids=true, to_apply=%region_14.19 | all-reduce | flops 1344 | bytes 10752 | tf_op jit(solution)/shard_map/psum | solution.py:92
  197.5 77.2 %all-reduce = (f32[32,32]{1,0:T(8,128)S(1)}, f32[32,8]{0,1:T(8,128)S(1)}, f32[8,8]{0,1:T(8,128)S(1)}) all-reduce(f32[32,32]{1,0:T(8,128)S(1)} %get-tuple-element.14, f32[32,8]{0,1:T(8,128)S(1)} %get-tuple-element.15, f32[8,8]{0,1:T(8,128)S(1)} %get-tuple-element.16), channel_id=1, replica_groups=mesh['dom'=16,'spin'=2] {'dom'}, use_global_device_ids=true, to_apply=%region_15.20 | all-reduce | flops 1344 | bytes 10752 | tf_op jit(solution)/shard_map/psum | solution.py:91
  275.0 1.3 convolution_subtract_fusion
  276.8 0.7 cholesky.55
  277.6 0.6 compare_reduce_fusion
  278.3 0.6 fusion.59
  278.9 0.7 pad_maximum_fusion.9
  279.6 0.6 custom-call.7
  280.2 1.4 convolution_bitcast_fusion
  (51 shorter events, 2.5 us)
Async XLA Ops:
  0.6 15.4 %copy-start = (bf16[8,128,128]{2,1,0:T(8,128)(2,1)S(1)}, bf16[8,128,128]{2,1,0:T(8,128)(2,1)}, u32[]{:S(2)}) copy-start(bf16[8,128,128]{2,1,0:T(8,128)(2,1)} %param.19) | copy-start | bytes 786436
  1.8 51.3 %collective-permute-start.2 = (bf16[8,128,128]{2,1,0:T(8,128)(2,1)S(1)}, bf16[8,128,128]{2,1,0:T(8,128)(2,1)S(1)}, u32[]{:S(2)}, u32[]{:S(2)}) collective-permute-start(bf16[8,128,128]{2,1,0:T(8,128)(2,1)S(1)} %bitcast.137), channel_id=1, source_target_pairs={{0,1},{1,0},{2,3},{3,2},{4,5},{5,4},{6,7},{7,6},{8,9},{9,8},{10,11... | collective-permute-start | bytes 786440 | tf_op jit(solution)/shard_map/ppermute | solution.py:33
  2.4 13.6 %collective-permute-start = (bf16[8,8,128]{2,1,0:T(8,128)(2,1)S(1)}, bf16[8,8,128]{2,1,0:T(8,128)(2,1)S(1)}, u32[]{:S(2)}, u32[]{:S(2)}) collective-permute-start(bf16[8,8,128]{2,1,0:T(8,128)(2,1)S(1)} %get-tuple-element.24), channel_id=1, source_target_pairs={{0,2},{2,4},{4,6},{6,8},{8,10},{10,12},{12,14},{14,16},{16,18},{18... | collective-permute-start | bytes 49160 | tf_op jit(solution)/shard_map/ppermute | solution.py:17
  5.0 11.1 %collective-permute-start.1 = (bf16[8,8,128]{2,1,0:T(8,128)(2,1)S(1)}, bf16[8,8,128]{2,1,0:T(8,128)(2,1)S(1)}, u32[]{:S(2)}, u32[]{:S(2)}) collective-permute-start(bf16[8,8,128]{2,1,0:T(8,128)(2,1)S(1)} %get-tuple-element.25), channel_id=1, source_target_pairs={{2,0},{4,2},{6,4},{8,6},{10,8},{12,10},{14,12},{16,14},{18,16},{20... | collective-permute-start | bytes 49160 | tf_op jit(solution)/shard_map/ppermute | solution.py:19
  43.9 11.0 %copy-start.1 = (f32[1,8,16384]{2,1,0:T(8,128)S(1)}, f32[1,8,16384]{2,1,0:T(8,128)}, u32[]{:S(2)}) copy-start(f32[1,8,16384]{2,1,0:T(8,128)} %param.16) | copy-start | bytes 1572868
  43.9 11.0 %copy-start.4 = (f32[1,16384]{1,0:T(1,128)S(1)}, f32[1,16384]{1,0:T(1,128)}, u32[]{:S(2)}) copy-start(f32[1,16384]{1,0:T(1,128)} %param.18) | copy-start | bytes 196612
  53.3 4.0 %copy-start.2 = (f32[1,16,16384]{2,1,0:T(8,128)S(1)}, f32[1,16,16384]{2,1,0:T(8,128)}, u32[]{:S(2)}) copy-start(f32[1,16,16384]{2,1,0:T(8,128)} %param.17) | copy-start | bytes 3145732
  54.9 4.0 %copy-start.5 = (f32[24,24]{1,0:T(8,128)S(1)}, f32[24,24]{1,0:T(8,128)}, u32[]{:S(2)}) copy-start(f32[24,24]{1,0:T(8,128)} %fusion.1) | copy-start | bytes 6916
  141.1 133.9 %copy-start.3 = (f32[8,16384]{1,0:T(8,128)}, f32[8,16384]{1,0:T(8,128)S(1)}, u32[]{:S(2)}) copy-start(f32[8,16384]{1,0:T(8,128)S(1)} %fusion.47) | copy-start | bytes 1572868
  141.2 46.8 %collective-permute-start.5 = (bf16[8,128,128]{2,0,1:T(8,128)(2,1)S(1)}, bf16[8,128,128]{2,0,1:T(8,128)(2,1)}, u32[]{:S(2)}, u32[]{:S(2)}) collective-permute-start(bf16[8,128,128]{2,0,1:T(8,128)(2,1)S(1)} %convert_bitcast_fusion), channel_id=1, source_target_pairs={{0,1},{1,0},{2,3},{3,2},{4,5},{5,4},{6,7},{7,6},{8,9},{9,8},{10,11... | collective-permute-start | bytes 786440 | tf_op jit(solution)/shard_map/ppermute | solution.py:33
  143.7 7.3 %collective-permute-start.3 = (bf16[8,8,128]{2,1,0:T(8,128)(2,1)S(1)}, bf16[8,8,128]{2,1,0:T(8,128)(2,1)S(1)}, u32[]{:S(2)}, u32[]{:S(2)}) collective-permute-start(bf16[8,8,128]{2,1,0:T(8,128)(2,1)S(1)} %get-tuple-element.22), channel_id=1, source_target_pairs={{0,2},{2,4},{4,6},{6,8},{8,10},{10,12},{12,14},{14,16},{16,18},{18... | collective-permute-start | bytes 49160 | tf_op jit(solution)/shard_map/ppermute | solution.py:17
  143.7 7.3 %collective-permute-start.4 = (bf16[8,8,128]{2,1,0:T(8,128)(2,1)S(1)}, bf16[8,8,128]{2,1,0:T(8,128)(2,1)S(1)}, u32[]{:S(2)}, u32[]{:S(2)}) collective-permute-start(bf16[8,8,128]{2,1,0:T(8,128)(2,1)S(1)} %get-tuple-element.23), channel_id=1, source_target_pairs={{2,0},{4,2},{6,4},{8,6},{10,8},{12,10},{14,12},{16,14},{18,16},{20... | collective-permute-start | bytes 49160 | tf_op jit(solution)/shard_map/ppermute | solution.py:19
  178.9 10.8 %copy-start.7 = (pred[128]{0:T(512)(128)(4,1)S(1)}, pred[128]{0:T(512)(128)(4,1)}, u32[]{:S(2)}) copy-start(pred[128]{0:T(512)(128)(4,1)} %get-tuple-element.20) | copy-start | bytes 388
  190.9 3.2 %copy-start.6 = (f32[32,32]{1,0:T(8,128)S(1)}, f32[32,32]{1,0:T(8,128)}, u32[]{:S(2)}) copy-start(f32[32,32]{1,0:T(8,128)} %fusion.3) | copy-start | bytes 12292
